TPU v7x, 256 devices: a whole 4x4x8 slice. The times are simulated.
256 devices in a mesh: blk: 64 (over z, x, y_lo), lane: 4 (over y_hi, core).
Axes of the slice: x: 4, y: 4 (y_hi: 2, y_lo: 2; y = y_hi * 2 + y_lo), z: 8, core: 2. Of those that a mesh axis runs over, the one named last changes fastest.
Arguments:
- features: float32 [98304, 512], P(('blk', 'lane')), may hold values from -6 to 6
- weight: float32 [512, 512], replicated, may hold values from -0.25 to 0.25
- hub_values: float32 [3, 98304, 1536], P(None, 'blk', 'lane'), may hold values from -0.125 to 0.125
- hub_mask: int32 [3, 768, 12], P(None, 'blk', 'lane'), may hold values 0 or 1
- tail_values: float32 [4608, 128, 128], P(('blk', 'lane')), may hold values from -0.21875 to 0.21875
- tail_reader: int32 [4608], P(('blk', 'lane')), may hold values from 0 to 63, as said below
- tail_target: int32 [4608], P(('blk', 'lane')), may hold values from 0 to 2
Outputs:
- activations: float32 [98304, 512], P(('blk', 'lane'))
Inputs may be any that keep to these rules, and one draw needn't show every extreme that they name: `tail_reader`: A tail tile of a device in slab b names a reader (b + o) mod 64 with 1 <= o <= 32; within one device's 18 tail tiles no reader is named more than 1 times, and on every device some reader is named exactly 1 times.
All inputs are finite; a program needn't handle non-finite values. No bound on the sum of `hub_mask` on one device may be relied on, other than what follows from the above.
Results may differ from a plain program's by a relative error of at most 0.0003.
Values sent between devices are 32-bit elements; how exact they have to be, the bound alone decides.
A program may use at most 128 MiB of HBM per device.

v0:
```python
import jax
import jax.numpy as jnp
from jax import lax
from jax.sharding import PartitionSpec as P

BLOCK = 128
TILES = 6


def passed_along(value, axis, steps):
    count = lax.axis_size(axis)
    pairs = [(source, (source + steps) % count) for source in range(count)]
    return lax.ppermute(value, axis, pairs)


def per_device(features, weight, hub_values, hub_mask, tail_values, tail_reader, tail_target):
    highest = lax.Precision.HIGHEST
    row_count, feat_width = features.shape
    stop_count = hub_values.shape[0]
    blk_count = lax.axis_size("blk")
    block_count = row_count // BLOCK
    tail_count = tail_reader.shape[0]
    reach_count = blk_count // 2
    slot_cap = (tail_count + reach_count - 1) // reach_count
    dense_vals = hub_values * jnp.repeat(
        jnp.repeat(hub_mask.astype(jnp.float32), BLOCK, 1), BLOCK, 2
    )
    shifted = [features]
    current = features
    for stop_idx in range(1, stop_count):
        current = passed_along(current, "blk", 1)
        shifted.append(current)
    running = jnp.zeros((lax.axis_size("lane") * row_count, feat_width), jnp.float32)
    for stop_idx in range(stop_count):
        rows_here = dense_vals[stop_idx]
        running = running + jnp.dot(
            rows_here, shifted[stop_idx], precision=highest, preferred_element_type=jnp.float32
        )
    hub_agg = lax.psum_scatter(running, "lane", scatter_dimension=0, tiled=True)
    block_feats = features.reshape(block_count, BLOCK, feat_width)
    tile_vals = tail_values.reshape(block_count, TILES, BLOCK, BLOCK)
    products = jnp.einsum("kjab,kbf->kjaf", tile_vals, block_feats, precision=highest).reshape(
        tail_count, BLOCK * feat_width
    )
    block_ids = jnp.arange(block_count, dtype=jnp.int32)
    tail_order = jnp.arange(tail_count, dtype=jnp.int32)
    same_reader = (tail_reader[:, None] == tail_reader[None, :]) & (
        tail_order[None, :] < tail_order[:, None]
    )
    earlier_same = same_reader.astype(jnp.int32).sum(1)
    slot_index = tail_reader * slot_cap + earlier_same
    outgoing = (
        jnp.zeros((blk_count * slot_cap, BLOCK * feat_width), jnp.float32)
        .at[slot_index]
        .set(products)
    )
    out_targets = (
        jnp.full((blk_count * slot_cap,), block_count, jnp.int32).at[slot_index].set(tail_target)
    )
    incoming, in_targets = (
        lax.all_to_all(
            outgoing.reshape(blk_count, slot_cap, BLOCK * feat_width),
            "blk",
            split_axis=0,
            concat_axis=0,
            tiled=True,
        ),
        lax.all_to_all(
            out_targets.reshape(blk_count, slot_cap), "blk", split_axis=0, concat_axis=0, tiled=True
        ),
    )
    incoming = incoming.reshape(blk_count * slot_cap, BLOCK * feat_width)
    in_targets = in_targets.reshape(-1)
    in_pick = (in_targets[None, :] == block_ids[:, None]).astype(jnp.float32)
    tail_rows = jnp.dot(in_pick, incoming, precision=highest, preferred_element_type=jnp.float32)
    combined = hub_agg + tail_rows.reshape(row_count, feat_width)
    return jnp.maximum(
        jnp.dot(combined, weight, precision=highest, preferred_element_type=jnp.float32), 0.0
    )


def solution(mesh):
    return jax.shard_map(
        per_device,
        mesh=mesh,
        in_specs=(
            P(("blk", "lane"), None),
            P(),
            P(None, "blk", "lane"),
            P(None, "blk", "lane"),
            P(("blk", "lane"), None, None),
            P(("blk", "lane")),
            P(("blk", "lane")),
        ),
        out_specs=P(("blk", "lane"), None),
        check_vma=False,
    )
```

profile of v0, /device:TPU:16, one launch (start us, length us, event | category | flops | bytes accessed | tf_op | source)
XLA Modules:
  0.0 599.4 jit_solution(16491328937392838033)
XLA Ops:
  6.5 0.0 copy-start
  6.5 0.9 convert_reduce_fusion
  7.5 0.7 compare_select_fusion
  8.2 0.8 scatter_custom_fusion
  8.9 0.7 copy.15
  9.6 12.7 %all-to-all-start = ((s32[64,1,1]{2,1,0:T(1,128)}), s32[64,1,1]{2,1,0:T(1,128)S(1)}, u32[]{:S(2)}, u32[]{:S(2)}) async-start(s32[64,1,1]{2,1,0:T(1,128)} %copy.15), calls=%async_computation.1 | async-start | bytes 65536 | tf_op jit(solution)/shard_map/all_to_all | solution.py:68
  22.3 0.0 copy-done
  22.3 5.1 fusion.9
  27.4 0.9 pad
  28.3 6.3 %copy.18 = f32[3,8,128,512]{3,1,2,0:T(8,128)} copy(f32[3,8,128,512]{3,2,1,0:T(8,128)S(1)} %bitcast.35) | data formatting | bytes 12582912
  34.6 7.1 %broadcast_in_dim.25 = f32[64,65536]{1,0:T(8,128)} broadcast(f32[]{:T(128)} %constant.1.clone.1), dimensions={} | broadcast | bytes 16777220 | tf_op jit(solution)/shard_map/broadcast_in_dim | solution.py:53
  41.6 47.5 %scatter_fusion = f32[64,65536]{1,0:T(8,128)} fusion(f32[64,65536]{1,0:T(8,128)} %broadcast_in_dim.25, s32[18]{0:T(128)S(1)} %compare_select_fusion, f32[18,65536]{1,0:T(8,128)} %bitcast.34), kind=kCustom, calls=%fused_computation.1 | custom fusion | bytes 14155848 | tf_op jit(solution)/shard_map/scatter | solution.py:55
  89.2 15.0 %reshape.37 = f32[64,1,65536]{2,1,0:T(1,128)} reshape(f32[64,65536]{1,0:T(8,128)} %scatter_fusion) | data formatting | bytes 33554432 | tf_op jit(solution)/shard_map/reshape | solution.py:62
  104.2 0.0 copy-start.2
  104.2 0.0 all-to-all-done
  104.2 12.7 %all-to-all-start.1 = ((f32[64,1,65536]{2,1,0:T(1,128)}), f32[64,1,65536]{2,1,0:T(1,128)}, u32[]{:S(2)}, u32[]{:S(2)}) async-start(f32[64,1,65536]{2,1,0:T(1,128)} %reshape.37), calls=%async_computation.2 | async-start | bytes 33554432 | tf_op jit(solution)/shard_map/all_to_all | solution.py:61
  116.9 0.0 copy-start.3
  116.9 0.0 reduce-scatter.2.cloned.1.call-start
  116.9 0.0 copy-done.2
  116.9 1.6 collective-permute-start
  118.5 8.1 %copy.14 = f32[3,1536,384]{1,2,0:T(8,128)} copy(f32[3,1536,384]{2,1,0:T(8,128)} %param.9) | data formatting | bytes 14155776 | tf_op args[2]
  126.6 0.0 copy-done.3
  126.7 0.1 broadcast_in_dim.10
  126.8 4.1 bitcast_multiply_fusion
  130.8 370.1 %collective-permute-done = f32[384,512]{1,0:T(8,128)S(1)} collective-permute-done((f32[384,512]{1,0:T(8,128)S(1)}, f32[384,512]{1,0:T(8,128)S(1)}, u32[]{:S(2)}, u32[]{:S(2)}) %collective-permute-start) | collective-permute-done | bytes 786464 | tf_op jit(solution)/shard_map/ppermute | solution.py:13
  500.9 0.4 collective-permute-start.1
  501.3 5.3 fusion.3
  506.6 5.3 convolution_add_fusion.1
  511.9 10.5 %collective-permute-done.1 = f32[384,512]{1,0:T(8,128)S(1)} collective-permute-done((f32[384,512]{1,0:T(8,128)S(1)}, f32[384,512]{1,0:T(8,128)S(1)}, u32[]{:S(2)}, u32[]{:S(2)}) %collective-permute-start.1) | collective-permute-done | bytes 786464 | tf_op jit(solution)/shard_map/ppermute | solution.py:13
  522.4 7.0 %convolution_add_fusion = f32[1536,512]{1,0:T(8,128)} fusion(f32[1536,512]{1,0:T(8,128)S(1)} %convolution_add_fusion.1, f32[384,512]{1,0:T(8,128)S(1)} %collective-permute-done.1, f32[3,1536,384]{1,2,0:T(8,128)S(1)} %bitcast_multiply_fusion), kind=kOutput, calls=%fused_computation.6 | convolution fusion | flops 3624665088 | bytes 9437184 | tf_op jit(solution)/shard_map/dot_general | solution.py:36
  529.4 0.0 reduce-scatter.2.cloned.1.call-update
  529.4 1.2 reduce
  530.6 0.0 all-to-all-done.1
  530.6 0.0 copy-start.1
  530.7 20.0 %fusion = f32[3,65536]{1,0:T(4,128)S(1)} fusion(f32[64,1,65536]{2,1,0:T(1,128)} %all-to-all-done.1, s32[64]{0:T(128)S(1)} %reduce), kind=kOutput, calls=%fused_computation.2 | convolution fusion | flops 150995136 | bytes 17563904 | tf_op jit(solution)/shard_map/dot_general | solution.py:75
  550.6 0.6 reshape.39
  551.2 37.3 %reduce-scatter.2.cloned.1.call-done = f32[384,512]{1,0:T(8,128)} async-done(((f32[1536,512]{1,0:T(8,128)}), f32[384,512]{1,0:T(8,128)}) %reduce-scatter.2.cloned.1.call-update) | async-done | bytes 786448 | tf_op jit(solution)/shard_map/reduce_scatter | solution.py:39
  588.6 3.8 convolution_maximum_fusion
  592.4 0.0 copy-done.1
  (2 shorter events, 0.0 us)
Async XLA Ops:
  6.5 15.8 %copy-start = (f32[18,128,128]{2,1,0:T(8,128)S(1)}, f32[18,128,128]{2,1,0:T(8,128)}, u32[]{:S(2)}) copy-start(f32[18,128,128]{2,1,0:T(8,128)} %param.11) | copy-start | bytes 3538948
  9.6 94.5 %all-to-all-start = ((s32[64,1,1]{2,1,0:T(1,128)}), s32[64,1,1]{2,1,0:T(1,128)S(1)}, u32[]{:S(2)}, u32[]{:S(2)}) async-start(s32[64,1,1]{2,1,0:T(1,128)} %copy.15), calls=%async_computation.1 | async-start | bytes 65536 | tf_op jit(solution)/shard_map/all_to_all | solution.py:68
  104.2 12.8 %copy-start.2 = (f32[384,512]{1,0:T(8,128)S(1)}, f32[384,512]{1,0:T(8,128)}, u32[]{:S(2)}) copy-start(f32[384,512]{1,0:T(8,128)} %param.7) | copy-start | bytes 2359300
  104.2 426.5 %all-to-all-start.1 = ((f32[64,1,65536]{2,1,0:T(1,128)}), f32[64,1,65536]{2,1,0:T(1,128)}, u32[]{:S(2)}, u32[]{:S(2)}) async-start(f32[64,1,65536]{2,1,0:T(1,128)} %reshape.37), calls=%async_computation.2 | async-start | bytes 33554432 | tf_op jit(solution)/shard_map/all_to_all | solution.py:61
  116.9 9.8 %copy-start.3 = (s32[3,12,3]{1,2,0:T(4,128)S(1)}, s32[3,12,3]{1,2,0:T(4,128)}, u32[]{:S(2)}) copy-start(s32[3,12,3]{1,2,0:T(4,128)} %param.10) | copy-start | bytes 1300
  116.9 471.7 %reduce-scatter.2.cloned.1.call-start = ((), (), s32[]{:S(2)}) async-start(), calls=%async_computation.3 | async-start | bytes 3932160 | tf_op jit(solution)/shard_map/reduce_scatter | solution.py:39
  116.9 384.0 %collective-permute-start = (f32[384,512]{1,0:T(8,128)S(1)}, f32[384,512]{1,0:T(8,128)S(1)}, u32[]{:S(2)}, u32[]{:S(2)}) collective-permute-start(f32[384,512]{1,0:T(8,128)S(1)} %copy-done.2), channel_id=1, source_target_pairs={{0,4},{4,8},{8,12},{12,16},{16,20},{20,24},{24,28},{28,32},{32,36}... | collective-permute-start | bytes 2359304 | tf_op jit(solution)/shard_map/ppermute | solution.py:13
  500.9 21.5 %collective-permute-start.1 = (f32[384,512]{1,0:T(8,128)S(1)}, f32[384,512]{1,0:T(8,128)S(1)}, u32[]{:S(2)}, u32[]{:S(2)}) collective-permute-start(f32[384,512]{1,0:T(8,128)S(1)} %collective-permute-done), channel_id=1, source_target_pairs={{0,4},{4,8},{8,12},{12,16},{16,20},{20,24},{24,28},{28,32},{32,36}... | collective-permute-start | bytes 2359304 | tf_op jit(solution)/shard_map/ppermute | solution.py:13
  530.6 61.7 %copy-start.1 = (f32[18,128,128]{2,1,0:T(8,128)S(1)}, f32[18,128,128]{2,1,0:T(8,128)}, u32[]{:S(2)}) copy-start(f32[18,128,128]{2,1,0:T(8,128)} %param.11) | copy-start | bytes 3538948
Sparse Core Ops, SparseCore 0:
  529.5 58.9 reduce-scatter.1
where the time goes:
time: 611 us; the launch traced here: 599 us
  waiting for transfers between devices  418 us (68%)
  local copies, waits for them, and re-layouts  87.1 us (14%)
  matrix products  46.4 us (8%)
  starting transfers between devices  27.4 us (4%)
  between operations  13.7 us (2%)
  other arithmetic  6.89 us (1%)
    ppermute x2, waiting for transfers between devices, passed_along(): return lax.ppermute(value, axis, pairs)  381 us
    scatter x1, local copies, waits for them, and re-layouts, per_device(): outgoing = jnp.zeros((blk_count * slot_cap, BLOCK * feat_width), jnp.floa...  47.5 us
    reduce_scatter x1, waiting for transfers between devices, per_device(): hub_agg = lax.psum_scatter(running, 'lane', scatter_dimension=0, tiled=True)  37.3 us
    dot_general x1, matrix products, per_device(): jnp.dot(in_pick, incoming, precision=highest, preferred_element_type=jnp....  20 us
    dot_general x3, matrix products, per_device(): jnp.dot(rows_here, shifted[stop_idx], precision=highest, preferred_elemen...  17.6 us
    unnamed x11, local copies, waits for them, and re-layouts  15.3 us
    reshape x1, local copies, waits for them, and re-layouts, per_device(): outgoing.reshape(blk_count, slot_cap, BLOCK * feat_width)  15 us
    all_to_all x1, starting transfers between devices, per_device(): lax.all_to_all(outgoing.reshape(blk_count, slot_cap, BLOCK * feat_width),...  12.7 us
  transfers between devices with their start and end apart: 5, of which 3 were waited for; matrix products, arithmetic and copies ran while one was open for 22% of the time, Pallas kernels for 0%

commit v1 on v0

v1 whole, which is shorter than its diff:
```python
import functools

import jax
import jax.numpy as jnp
from jax import lax
from jax.experimental import pallas as pl
from jax.experimental.pallas import tpu as pltpu
from jax.sharding import PartitionSpec as P

MESH = pl.DeviceIdType.MESH
BLOCK = 128
TILES = 6
TAILS = 18
NZ, NX, NY = 8, 4, 2
PLANE = NX * NY
WIN = 4
ROWS, FEAT = 384, 512
NC = 4
N = FEAT // NC
SPLIT = 192
BF = jnp.bfloat16
F32 = jnp.float32


def halves(value):
    hi = value.astype(BF)
    return hi, (value - hi.astype(F32)).astype(BF)


def dot3(ah, al, bh, bl):
    def dot(a, b):
        return jnp.dot(a, b, preferred_element_type=F32)

    return dot(ah, bh) + (dot(ah, bl) + dot(al, bh))


def kernel(
    feat_hbm, weight_hbm, hub_hbm, tail_hbm, mask, slot_tile, meta,
    out,
    fbuf, fh, fl, tsend, trecv, tvals, mrecv, mscal, eh, el, rh, rl, hubv, ah, al, hh, hl,
    run, crecv, hrecv, acc, zrecv, wv, wh, wl,
    load_sem, gs, gr, ts, tr, ms, mr, cs, cr, hs, hr, zs, zr, ws, wr,
):
    blk, lane = lax.axis_index("blk"), lax.axis_index("lane")
    z, p = lax.div(blk, PLANE), lax.rem(blk, PLANE)
    x, y = lax.div(p, NY), lax.rem(p, NY)
    h, c = lax.div(lane, 2), lax.rem(lane, 2)

    def at(zz, pp, hh_=None, cc=None):
        hh_ = h if hh_ is None else hh_
        cc = c if cc is None else cc
        return {"blk": lax.rem(zz + NZ, NZ) * PLANE + pp, "lane": hh_ * 2 + cc}

    def pos(xx, yy):
        return lax.rem(xx + NX, NX) * NY + yy

    def remote(src, dst, send, recv, dev):
        return pltpu.make_async_remote_copy(
            src_ref=src, dst_ref=dst, send_sem=send, recv_sem=recv, device_id=dev, device_id_type=MESH
        )

    feat_in = [
        pltpu.make_async_copy(feat_hbm.at[:, pl.ds(n * N, N)], fbuf.at[n, p], load_sem.at[n]) for n in range(NC)
    ]
    tail_in = pltpu.make_async_copy(tail_hbm, tvals.at[pl.ds(0, TAILS)], load_sem.at[NC])
    hub_in = [pltpu.make_async_copy(hub_hbm.at[s], hubv.at[s], load_sem.at[NC + 1 + s]) for s in range(3)]
    weight_in = pltpu.make_async_copy(weight_hbm, wv, load_sem.at[NC + 4])
    meta_in = pltpu.make_async_copy(meta.at[p], mrecv.at[p], load_sem.at[NC + 5])
    feat_in[0].start()
    tail_in.start()
    meta_in.start()
    for copy in feat_in[1:] + hub_in + [weight_in]:
        copy.start()

    barrier = pltpu.get_barrier_semaphore()
    partners = [at(z, lax.rem(p + i, PLANE)) for i in range(1, PLANE)]
    partners += [at(z + 1, p), at(z - 1, p), at(z + 4, p), at(z, p, h, 1 - c), at(z, p, 1 - h, c)]
    for dev in partners:
        pl.semaphore_signal(barrier, inc=1, device_id=dev, device_id_type=MESH)
    pl.semaphore_wait(barrier, len(partners))

    yn, left, right = pos(x, 1 - y), pos(x - 1, y), pos(x + 1, y)
    right_yn = pos(x + 1, 1 - y)
    flows = [(p, yn), (p, right), (p, left), (yn, right), (yn, left), (left, right), (right_yn, left)]

    def gather(n, i):
        slot, dest = flows[i]
        return remote(fbuf.at[n, slot], fbuf.at[n, slot], gs.at[n, i], gr.at[n, i], at(z, dest))

    gathers = [[gather(n, i) for i in range(7)] for n in range(NC)]

    def first_sends(n):
        feat_in[n].wait()
        for i in range(3):
            gathers[n][i].start()

    wraps = [
        [
            remote(fbuf.at[n, 7 - i], fbuf.at[n, 8 + i], ws.at[n, i], wr.at[n, i], at(z + 1, p))
            for i in range(2)
        ]
        for n in range(NC)
    ]

    first_sends(0)

    tail_in.wait()
    tvals[TAILS] = jnp.zeros((BLOCK, BLOCK), F32)
    tile_copies, meta_copies = [], []
    for i in range(1, PLANE):
        q = lax.rem(p + i, PLANE)
        for j in range(WIN):
            tsend[q, j] = tvals[slot_tile[q * WIN + j]]
        tile_copies.append(remote(tsend.at[q], trecv.at[p], ts.at[i - 1], tr.at[i - 1], at(z, q)))
        meta_copies.append(remote(meta.at[q], mrecv.at[p], ms.at[i - 1], mr.at[i - 1], at(z, q)))
        tile_copies[-1].start()
        meta_copies[-1].start()
    for j in range(WIN):
        trecv[p, j] = tvals[slot_tile[p * WIN + j]]

    first_sends(1)

    for s in range(3):
        hub_in[s].wait()

        def hub_rows(i, carry):
            for jj in range(3):
                present = mask[s, i, jj].astype(F32)
                rows = pl.ds(pl.multiple_of(i * BLOCK, BLOCK), BLOCK)
                hi, lo = halves(hubv[s, rows, jj * BLOCK:(jj + 1) * BLOCK] * present)
                cols = slice(s * ROWS + jj * BLOCK, s * ROWS + (jj + 1) * BLOCK)
                ah[rows, cols] = hi
                al[rows, cols] = lo
            return carry

        lax.fori_loop(0, 12, hub_rows, 0)
    weight_in.wait()
    for i in range(4):
        hi, lo = halves(wv[i * BLOCK:(i + 1) * BLOCK])
        wh[i * BLOCK:(i + 1) * BLOCK] = hi
        wl[i * BLOCK:(i + 1) * BLOCK] = lo

    order = ([4, 3, 2, 1], [1, 2, 3, 4])
    part = (slice(0, SPLIT), slice(SPLIT, ROWS))
    size = (SPLIT, ROWS - SPLIT)

    def chain(n, way, s):
        rows = pl.ds(0, size[way])
        src = acc.at[n, order[way][0], pl.ds(part[way].start, size[way])] if s == 0 else zrecv.at[n, way, s - 1, rows]
        zz = z + 1 if way == 0 else (z - 1 if s < 3 else z + 4)
        return remote(src, zrecv.at[n, way, s, rows], zs.at[n, way, s], zr.at[n, way, s], at(zz, p))

    chains = [[[chain(n, way, s) for s in range(4)] for way in range(2)] for n in range(NC)]

    def chain_step(n, s):
        for way in range(2):
            chains[n][way][s - 1].wait_recv()
            rows = slice(0, size[way])
            zrecv[n, way, s - 1, rows] = zrecv[n, way, s - 1, rows] + acc[n, order[way][s], part[way]]
            chains[n][way][s].start()

    def tail_product(n, d):
        for pp in range(PLANE):
            j = d - (p <= pp).astype(jnp.int32)
            k = mscal[pp, 0, jnp.clip(j, 0, WIN - 1)] + 3 * pp
            rh[pp * BLOCK:(pp + 1) * BLOCK] = fh[k]
            rl[pp * BLOCK:(pp + 1) * BLOCK] = fl[k]
        acc[n, d] = dot3(eh[d], el[d], rh[...], rl[...])

    def convert(n, slot):
        for i in range(3):
            hi, lo = halves(fbuf[n, slot, i * BLOCK:(i + 1) * BLOCK])
            fh[slot * 3 + i] = hi
            fl[slot * 3 + i] = lo

    slot1 = jnp.where(p >= 1, p - 1, 8)
    slot2 = jnp.where(p >= 2, p - 2, jnp.where(p == 1, 8, 9))

    core_copies = [
        remote(run.at[n, 1 - c], crecv.at[n], cs.at[n], cr.at[n], at(z, p, h, 1 - c)) for n in range(NC)
    ]
    half_rows = (pl.ds(0, ROWS // 2), pl.ds(ROWS // 2, ROWS // 2))
    half_copies = [
        [
            remote(run.at[n, c, 1 - h, half_rows[i]], hrecv.at[n, half_rows[i]], hs.at[n, i], hr.at[n, i], at(z, p, 1 - h, c))
            for i in range(2)
        ]
        for n in range(NC)
    ]

    def hub_product(n):
        for s, slot in enumerate((p, slot1, slot2)):
            for i in range(3):
                rows = slice(s * ROWS + i * BLOCK, s * ROWS + (i + 1) * BLOCK)
                hh[rows] = fh[slot * 3 + i]
                hl[rows] = fl[slot * 3 + i]

        def quarter(i, carry):
            rows = pl.ds(pl.multiple_of(i * ROWS, BLOCK), ROWS)
            run[n, lax.rem(i, 2), lax.div(i, 2)] = dot3(ah[rows], al[rows], hh[...], hl[...])
            return carry

        lax.fori_loop(0, 4, quarter, 0)
        core_copies[n].start()

    def hub_sum(n):
        core_copies[n].wait_recv()
        for i in range(2):
            run[n, c, i] = run[n, c, i] + crecv[n, i]
        for copy in half_copies[n]:
            copy.start()

    def finish(n):
        for way in range(2):
            chains[n][way][3].wait_recv()
        for copy in half_copies[n]:
            copy.wait_recv()
        for way in range(2):
            rows = part[way]
            total = (run[n, c, h, rows] + hrecv[n, rows]) + (acc[n, 0, rows] + zrecv[n, way, 3, 0:size[way]])
            hi, lo = halves(total)
            cols = slice(n * N, (n + 1) * N)
            value = dot3(hi, lo, wh[cols], wl[cols])
            if n > 0:
                value = out[rows] + value
            out[rows] = jnp.maximum(value, 0.0) if n == NC - 1 else value

    def build_tiles():
        meta_in.wait()
        for copy in meta_copies:
            copy.wait_recv()
        scal = pltpu.make_async_copy(mrecv, mscal, load_sem.at[NC + 6])
        scal.start()
        for copy in tile_copies:
            copy.wait_recv()
        scal.wait()

        def source(pp, carry):
            cols = pl.ds(pl.multiple_of(pp * BLOCK, BLOCK), BLOCK)
            none = pl.ds(0, ROWS)
            zero = jnp.zeros((ROWS, BLOCK), BF)
            empty = jnp.where(pp < p, 4, 0)
            eh[empty, none, cols] = zero
            el[empty, none, cols] = zero
            for j in range(WIN):
                d = j + (p <= pp).astype(jnp.int32)
                value = trecv[pp, j]
                target = mscal[pp, 1, j]
                for t in range(3):
                    hi, lo = halves(value * (target == t).astype(F32))
                    eh[d, t * BLOCK:(t + 1) * BLOCK, cols] = hi
                    el[d, t * BLOCK:(t + 1) * BLOCK, cols] = lo
            return carry

        lax.fori_loop(0, PLANE, source, 0)

    pending = []

    def serve(count=1):
        for _ in range(count):
            if pending:
                chain_step(*pending.pop(0))

    for n in range(NC):
        g = gathers[n]
        g[0].wait_recv()
        g[3].start()
        g[4].start()
        g[1].wait_recv()
        g[5].start()
        g[4].wait_recv()
        g[6].start()
        if n + 2 < NC:
            first_sends(n + 2)
        if n == 0:
            build_tiles()
        else:
            hub_sum(n - 1)
        serve()
        for i in (2, 3, 5, 6):
            g[i].wait_recv()
        for i in range(2):

            @pl.when(p < 2 - i)
            def _():
                wraps[n][i].start()

        lax.fori_loop(0, PLANE, lambda slot, carry: (convert(n, slot), carry)[1], 0)
        tail_product(n, 4)
        chains[n][0][0].start()
        tail_product(n, 1)
        chains[n][1][0].start()
        serve()
        tail_product(n, 3)
        tail_product(n, 2)
        serve()
        tail_product(n, 0)
        for i in range(2):

            @pl.when(p < 2 - i)
            def _():
                wraps[n][i].wait_recv()
                convert(n, 8 + i)

        hub_product(n)
        if n > 0:
            finish_before = n - 1
            while pending and pending[0][0] < finish_before:
                serve()
        pending.extend((n, s) for s in range(1, 4))

    hub_sum(NC - 1)
    done = 0
    while pending:
        step = pending[0]
        while done < step[0]:
            finish(done)
            done += 1
        serve()
    while done < NC:
        finish(done)
        done += 1

    for n in range(NC):
        for copy in gathers[n]:
            copy.wait_send()
        for way in range(2):
            for copy in chains[n][way]:
                copy.wait_send()
        core_copies[n].wait_send()
        for copy in half_copies[n]:
            copy.wait_send()
        for i in range(2):

            @pl.when(p < 2 - i)
            def _():
                wraps[n][i].wait_send()
    for copy in tile_copies + meta_copies:
        copy.wait_send()


def slot_tables(tail_reader, tail_target):
    blk = lax.axis_index("blk")
    z, p = blk // PLANE, blk % PLANE
    q = jnp.arange(PLANE * WIN, dtype=jnp.int32) // WIN
    j = jnp.arange(PLANE * WIN, dtype=jnp.int32) % WIN
    reader = ((z + j + (q <= p)) % NZ) * PLANE + q
    found = (tail_reader[None, :] == reader[:, None]).astype(jnp.int32)
    tiles = jnp.arange(TAILS, dtype=jnp.int32)
    tile = jnp.sum(found * (tiles - TAILS)[None, :], 1) + TAILS
    source = jnp.sum(found * (tiles // TILES)[None, :], 1)
    target = jnp.sum(found * tail_target[None, :], 1)
    meta = jnp.stack([source.reshape(PLANE, WIN), target.reshape(PLANE, WIN)], 1)
    meta = jnp.pad(meta, ((0, 0), (0, 6), (0, BLOCK - WIN)))
    return tile, meta


def per_device(features, weight, hub_values, hub_mask, tail_values, tail_reader, tail_target):
    tile, meta = slot_tables(tail_reader, tail_target)
    dma = pltpu.SemaphoreType.DMA
    any_ = pl.BlockSpec(memory_space=pl.ANY)
    vmem = pl.BlockSpec(memory_space=pltpu.VMEM)
    smem = pl.BlockSpec(memory_space=pltpu.SMEM)
    return pl.pallas_call(
        kernel,
        out_shape=jax.ShapeDtypeStruct((ROWS, FEAT), F32),
        in_specs=[any_, any_, any_, any_, smem, smem, vmem],
        out_specs=vmem,
        scratch_shapes=[
            pltpu.VMEM((NC, 10, ROWS, N), F32),
            pltpu.VMEM((30, BLOCK, N), BF),
            pltpu.VMEM((30, BLOCK, N), BF),
            pltpu.VMEM((PLANE, WIN, BLOCK, BLOCK), F32),
            pltpu.VMEM((PLANE, WIN, BLOCK, BLOCK), F32),
            pltpu.VMEM((TAILS + 1, BLOCK, BLOCK), F32),
            pltpu.VMEM((PLANE, 8, BLOCK), jnp.int32),
            pltpu.SMEM((PLANE, 8, BLOCK), jnp.int32),
            pltpu.VMEM((5, ROWS, PLANE * BLOCK), BF),
            pltpu.VMEM((5, ROWS, PLANE * BLOCK), BF),
            pltpu.VMEM((PLANE * BLOCK, N), BF),
            pltpu.VMEM((PLANE * BLOCK, N), BF),
            pltpu.VMEM((3, 4 * ROWS, ROWS), F32),
            pltpu.VMEM((4 * ROWS, 3 * ROWS), BF),
            pltpu.VMEM((4 * ROWS, 3 * ROWS), BF),
            pltpu.VMEM((3 * ROWS, N), BF),
            pltpu.VMEM((3 * ROWS, N), BF),
            pltpu.VMEM((NC, 2, 2, ROWS, N), F32),
            pltpu.VMEM((NC, 2, ROWS, N), F32),
            pltpu.VMEM((NC, ROWS, N), F32),
            pltpu.VMEM((NC, 5, ROWS, N), F32),
            pltpu.VMEM((NC, 2, 4, max(SPLIT, ROWS - SPLIT), N), F32),
            pltpu.VMEM((FEAT, FEAT), F32),
            pltpu.VMEM((FEAT, FEAT), BF),
            pltpu.VMEM((FEAT, FEAT), BF),
            dma((NC + 7,)),
            dma((NC, 7)),
            dma((NC, 7)),
            dma((7,)),
            dma((7,)),
            dma((7,)),
            dma((7,)),
            dma((NC,)),
            dma((NC,)),
            dma((NC, 2)),
            dma((NC, 2)),
            dma((NC, 2, 4)),
            dma((NC, 2, 4)),
            dma((NC, 2)),
            dma((NC, 2)),
        ],
        compiler_params=pltpu.CompilerParams(
            collective_id=0, has_side_effects=True, vmem_limit_bytes=62 << 20
        ),
    )(features, weight, hub_values, tail_values, hub_mask, tile, meta)


def solution(mesh):
    return jax.shard_map(
        per_device,
        mesh=mesh,
        in_specs=(
            P(("blk", "lane"), None),
            P(),
            P(None, "blk", "lane"),
            P(None, "blk", "lane"),
            P(("blk", "lane"), None, None),
            P(("blk", "lane")),
            P(("blk", "lane")),
        ),
        out_specs=P(("blk", "lane"), None),
        check_vma=False,
    )
```

time: 611 us -> 173 us (0.28); the launches traced: 599 us -> 173 us
  waiting for transfers between devices: 418 us -> 0 us
  Pallas kernels: 0 us -> 167 us
  local copies, waits for them, and re-layouts: 87.1 us -> 4.22 us
  matrix products: 46.4 us -> 0 us
  starting transfers between devices: 27.4 us -> 0 us
  between operations: 13.7 us -> 0.03 us
    ppermute x2 -> x0, waiting for transfers between devices: 381 us -> none  [passed_along(): return lax.ppermute(value, axis, pairs)]
    pallas_call x0 -> x1, Pallas kernels: none -> 167 us  [per_device(): pl.pallas_call(kernel, out_shape=jax.ShapeDtypeStruct((ROWS, FEAT), F32),...]
    scatter x2 -> x0, local copies, waits for them, and re-layouts: 48.3 us -> none  [the longest x1 47.5 us: per_device(): outgoing = jnp.zeros((blk_count * slot_cap, BLOCK * feat_width), jnp.floa...]
    dot_general x6 -> x0, matrix products: 46.4 us -> none  [the longest x1 20 us: per_device(): jnp.dot(in_pick, incoming, precision=highest, preferred_element_type=jnp....]
    reduce_scatter x1 -> x0, waiting for transfers between devices: 37.3 us -> none  [per_device(): hub_agg = lax.psum_scatter(running, 'lane', scatter_dimension=0, tiled=True)]
    all_to_all x2 -> x0, starting transfers between devices: 25.4 us -> none  [the longest x1 12.7 us: per_device(): lax.all_to_all(outgoing.reshape(blk_count, slot_cap, BLOCK * feat_width),...]
    reshape x3 -> x0, local copies, waits for them, and re-layouts: 15.6 us -> none  [the longest x1 15 us: per_device(): outgoing.reshape(blk_count, slot_cap, BLOCK * feat_width)]
    unnamed x11 -> x2, local copies, waits for them, and re-layouts: 15.3 us -> 3.45 us
  transfers between devices with their start and end apart: 5 -> 0, of which waited for: 3 -> 0; matrix products, arithmetic and copies ran while one was open for 22% -> 0% of each run, Pallas kernels for 0% -> 0%
where the time goes in v1:
time: 173 us
  Pallas kernels  167 us (97%)
  local copies, waits for them, and re-layouts  4.22 us (2%)
    pallas_call x1, Pallas kernels, per_device(): pl.pallas_call(kernel, out_shape=jax.ShapeDtypeStruct((ROWS, FEAT), F32),...  167 us

profile of v1, /device:TPU:16, one launch (start us, length us, event | category | flops | bytes accessed | tf_op | source)
XLA Modules:
  0.0 172.9 jit_solution(7819630504842229467)
XLA Ops:
  0.0 0.8 fusion.1
  0.8 0.5 broadcast_add_fusion.slot_tile
  1.3 0.1 stack_reshape.6
  1.4 0.1 stack_reshape.7
  1.5 0.6 pad.4.meta
  2.1 1.4 copy.16.mask
  3.5 167.3 %shard_map.73 = f32[384,512]{1,0:T(8,128)} custom-call(f32[384,512]{1,0:T(8,128)} %feat_hbm.1, f32[512,512]{1,0:T(8,128)} %weight_hbm.1, f32[3,1536,384]{2,1,0:T(8,128)} %hub_hbm.1, f32[18,128,128]{2,1,0:T(8,128)} %tail_hbm.1, s32[3,12,3]{2,1,0:T(8,128)} %copy.16.mask, s32[32]{0:T(128)} %broadcast_add_fusion.slot_tile, s32[8,8,128]{2,1,0:T(8,128)} %pad.4.meta), custom_call_target="tpu_custom_call" | custom-call | tf_op jit(solution)/shard_map/pallas_call | solution.py:364
  170.8 2.1 %copy.18 = f32[384,512]{1,0:T(8,128)} copy(f32[384,512]{1,0:T(8,128)} %shard_map.73) | data formatting | bytes 1572864
  (3 shorter events, 0.0 us)

commit v2 on v1

--- a/solution.py
+++ b/solution.py
@@ -17,7 +17,7 @@
 ROWS, FEAT = 384, 512
 NC = 4
 N = FEAT // NC
-SPLIT = 192
+SPLIT = 128
 BF = jnp.bfloat16
 F32 = jnp.float32
 
@@ -34,10 +34,15 @@
     return dot(ah, bh) + (dot(ah, bl) + dot(al, bh))
 
 
+def dot_pair(ah, al, pair):
+    both = jnp.dot(ah, pair, preferred_element_type=F32)
+    return (both[:, :N] + both[:, N:]) + jnp.dot(al, pair[:, :N], preferred_element_type=F32)
+
+
 def kernel(
     feat_hbm, weight_hbm, hub_hbm, tail_hbm, mask, slot_tile, meta,
     out,
-    fbuf, fh, fl, tsend, trecv, tvals, mrecv, mscal, eh, el, rh, rl, hubv, ah, al, hh, hl,
+    fbuf, fpair, tsend, tmid, trecv, tvals, mrecv, mscal, eh, el, rpair, hubv, ah, al, hpair,
     run, crecv, hrecv, acc, zrecv, wv, wh, wl,
     load_sem, gs, gr, ts, tr, ms, mr, cs, cr, hs, hr, zs, zr, ws, wr,
 ):
@@ -95,32 +100,70 @@
             gathers[n][i].start()
 
     wraps = [
-        [
-            remote(fbuf.at[n, 7 - i], fbuf.at[n, 8 + i], ws.at[n, i], wr.at[n, i], at(z + 1, p))
-            for i in range(2)
-        ]
-        for n in range(NC)
+        remote(fbuf.at[n, 6 + y], fbuf.at[n, 9 - y], ws.at[n, 0], wr.at[n, 0], at(z + 1, p)) for n in range(NC)
     ]
+    wraps_on = [remote(fbuf.at[n, 8], fbuf.at[n, 8], ws.at[n, 1], wr.at[n, 1], at(z, yn)) for n in range(NC)]
 
     first_sends(0)
 
     tail_in.wait()
     tvals[TAILS] = jnp.zeros((BLOCK, BLOCK), F32)
-    tile_copies, meta_copies = [], []
+    meta_copies = []
     for i in range(1, PLANE):
         q = lax.rem(p + i, PLANE)
+        meta_copies.append(remote(meta.at[q], mrecv.at[p], ms.at[i - 1], mr.at[i - 1], at(z, q)))
+        meta_copies[-1].start()
+    steps = (1, 3, 2)
+    cross, direct, onward = [], [], []
+
+    def fill(q):
         for j in range(WIN):
             tsend[q, j] = tvals[slot_tile[q * WIN + j]]
-        tile_copies.append(remote(tsend.at[q], trecv.at[p], ts.at[i - 1], tr.at[i - 1], at(z, q)))
-        meta_copies.append(remote(meta.at[q], mrecv.at[p], ms.at[i - 1], mr.at[i - 1], at(z, q)))
-        tile_copies[-1].start()
-        meta_copies[-1].start()
+
+    for i, dx in enumerate(steps + (0,)):
+        q = pos(x + dx, 1 - y)
+        fill(q)
+        landing = tmid.at[lax.rem(x + dx, NX)] if dx else trecv.at[p]
+        cross.append(remote(tsend.at[q], landing, ts.at[0, i], tr.at[0, i], at(z, yn)))
+        cross[-1].start()
+    for i, dx in enumerate(steps):
+        q = pos(x + dx, y)
+        fill(q)
+        direct.append(remote(tsend.at[q], trecv.at[p], ts.at[1, i], tr.at[1, i], at(z, q)))
+        direct[-1].start()
+        onward.append(remote(tmid.at[lax.rem(x + dx, NX)], trecv.at[yn], ts.at[2, i], tr.at[2, i], at(z, q)))
+
+    def pass_tile(i):
+        cross[i].wait_recv()
+        onward[i].start()
+
     for j in range(WIN):
         trecv[p, j] = tvals[slot_tile[p * WIN + j]]
 
-    first_sends(1)
-
-    for s in range(3):
+    def wrap_send(n):
+        @pl.when(p < 2)
+        def _():
+            wraps[n].start()
+
+    def wrap_forward(n):
+        @pl.when(p == 1)
+        def _():
+            wraps[n].wait_recv()
+            wraps_on[n].start()
+
+    def second_sends(n):
+        gathers[n][0].wait_recv()
+        gathers[n][3].start()
+        gathers[n][4].start()
+        gathers[n][1].wait_recv()
+        wrap_send(n)
+        gathers[n][5].start()
+
+    def third_send(n):
+        gathers[n][4].wait_recv()
+        gathers[n][6].start()
+
+    def hub_tiles(s):
         hub_in[s].wait()
 
         def hub_rows(i, carry):
@@ -134,6 +177,17 @@
             return carry
 
         lax.fori_loop(0, 12, hub_rows, 0)
+
+    second_sends(0)
+    hub_tiles(0)
+    pass_tile(0)
+    third_send(0)
+    first_sends(1)
+    hub_tiles(1)
+    pass_tile(1)
+    hub_tiles(2)
+    pass_tile(2)
+    wrap_forward(0)
     weight_in.wait()
     for i in range(4):
         hi, lo = halves(wv[i * BLOCK:(i + 1) * BLOCK])
@@ -163,18 +217,41 @@
         for pp in range(PLANE):
             j = d - (p <= pp).astype(jnp.int32)
             k = mscal[pp, 0, jnp.clip(j, 0, WIN - 1)] + 3 * pp
-            rh[pp * BLOCK:(pp + 1) * BLOCK] = fh[k]
-            rl[pp * BLOCK:(pp + 1) * BLOCK] = fl[k]
-        acc[n, d] = dot3(eh[d], el[d], rh[...], rl[...])
-
-    def convert(n, slot):
-        for i in range(3):
-            hi, lo = halves(fbuf[n, slot, i * BLOCK:(i + 1) * BLOCK])
-            fh[slot * 3 + i] = hi
-            fl[slot * 3 + i] = lo
-
-    slot1 = jnp.where(p >= 1, p - 1, 8)
-    slot2 = jnp.where(p >= 2, p - 2, jnp.where(p == 1, 8, 9))
+            rpair[pp * BLOCK:(pp + 1) * BLOCK] = fpair[k]
+        acc[n, d] = dot_pair(eh[d], el[d], rpair[...])
+
+    def convert(n):
+        def one(slot, carry):
+            for i in range(3):
+                hi, lo = halves(fbuf[n, slot, i * BLOCK:(i + 1) * BLOCK])
+                fpair[slot * 3 + i, :, :N] = hi
+                fpair[slot * 3 + i, :, N:] = lo
+            return carry
+
+        lax.fori_loop(0, PLANE, one, 0)
+
+    def hub_fill(n):
+        for s in range(3):
+            slot = jnp.maximum(p - s, 0)
+            for i in range(3):
+                hpair[s * ROWS + i * BLOCK:s * ROWS + (i + 1) * BLOCK] = fpair[slot * 3 + i]
+
+    def hub_fill_wrap(n):
+        def put(s, slot):
+            hi, lo = halves(fbuf[n, slot])
+            hpair[s * ROWS:(s + 1) * ROWS, :N] = hi
+            hpair[s * ROWS:(s + 1) * ROWS, N:] = lo
+
+        @pl.when(p == 0)
+        def _():
+            wraps_on[n].wait_recv()
+            put(1, 8)
+            wraps[n].wait_recv()
+            put(2, 9)
+
+        @pl.when(p == 1)
+        def _():
+            put(2, 8)
 
     core_copies = [
         remote(run.at[n, 1 - c], crecv.at[n], cs.at[n], cr.at[n], at(z, p, h, 1 - c)) for n in range(NC)
@@ -189,15 +266,9 @@
     ]
 
     def hub_product(n):
-        for s, slot in enumerate((p, slot1, slot2)):
-            for i in range(3):
-                rows = slice(s * ROWS + i * BLOCK, s * ROWS + (i + 1) * BLOCK)
-                hh[rows] = fh[slot * 3 + i]
-                hl[rows] = fl[slot * 3 + i]
-
         def quarter(i, carry):
             rows = pl.ds(pl.multiple_of(i * ROWS, BLOCK), ROWS)
-            run[n, lax.rem(i, 2), lax.div(i, 2)] = dot3(ah[rows], al[rows], hh[...], hl[...])
+            run[n, lax.rem(i, 2), lax.div(i, 2)] = dot_pair(ah[rows], al[rows], hpair[...])
             return carry
 
         lax.fori_loop(0, 4, quarter, 0)
@@ -225,101 +296,75 @@
                 value = out[rows] + value
             out[rows] = jnp.maximum(value, 0.0) if n == NC - 1 else value
 
-    def build_tiles():
-        meta_in.wait()
-        for copy in meta_copies:
-            copy.wait_recv()
-        scal = pltpu.make_async_copy(mrecv, mscal, load_sem.at[NC + 6])
-        scal.start()
-        for copy in tile_copies:
-            copy.wait_recv()
-        scal.wait()
-
-        def source(pp, carry):
-            cols = pl.ds(pl.multiple_of(pp * BLOCK, BLOCK), BLOCK)
-            none = pl.ds(0, ROWS)
-            zero = jnp.zeros((ROWS, BLOCK), BF)
-            empty = jnp.where(pp < p, 4, 0)
-            eh[empty, none, cols] = zero
-            el[empty, none, cols] = zero
-            for j in range(WIN):
-                d = j + (p <= pp).astype(jnp.int32)
-                value = trecv[pp, j]
-                target = mscal[pp, 1, j]
-                for t in range(3):
-                    hi, lo = halves(value * (target == t).astype(F32))
-                    eh[d, t * BLOCK:(t + 1) * BLOCK, cols] = hi
-                    el[d, t * BLOCK:(t + 1) * BLOCK, cols] = lo
-            return carry
-
-        lax.fori_loop(0, PLANE, source, 0)
-
-    pending = []
-
-    def serve(count=1):
-        for _ in range(count):
-            if pending:
-                chain_step(*pending.pop(0))
+    def build_tile(pp):
+        cols = pl.ds(pl.multiple_of(pp * BLOCK, BLOCK), BLOCK)
+        zero = jnp.zeros((ROWS, BLOCK), BF)
+        empty = jnp.where(pp < p, 4, 0)
+        eh[empty, pl.ds(0, ROWS), cols] = zero
+        el[empty, pl.ds(0, ROWS), cols] = zero
+        for j in range(WIN):
+            d = j + (p <= pp).astype(jnp.int32)
+            value = trecv[pp, j]
+            target = mscal[pp, 1, j]
+            hi = value.astype(BF).astype(F32)
+            lo = value - hi
+            for t in range(3):
+                keep = (target == t).astype(F32)
+                eh[d, t * BLOCK:(t + 1) * BLOCK, cols] = (hi * keep).astype(BF)
+                el[d, t * BLOCK:(t + 1) * BLOCK, cols] = (lo * keep).astype(BF)
+
+    meta_in.wait()
+    for copy in meta_copies:
+        copy.wait_recv()
+    scal = pltpu.make_async_copy(mrecv, mscal, load_sem.at[NC + 6])
+    scal.start()
+    scal.wait()
+    build_tile(p)
+    for i, dx in enumerate(steps):
+        direct[i].wait_recv()
+        build_tile(pos(x - dx, y))
+    cross[3].wait_recv()
+    build_tile(yn)
+    second_sends(1)
+    for i, dx in enumerate(steps):
+        onward[i].wait_recv()
+        build_tile(pos(x - dx, 1 - y))
 
     for n in range(NC):
-        g = gathers[n]
-        g[0].wait_recv()
-        g[3].start()
-        g[4].start()
-        g[1].wait_recv()
-        g[5].start()
-        g[4].wait_recv()
-        g[6].start()
+        if n > 0 and n + 1 < NC:
+            second_sends(n + 1)
         if n + 2 < NC:
             first_sends(n + 2)
-        if n == 0:
-            build_tiles()
-        else:
-            hub_sum(n - 1)
-        serve()
         for i in (2, 3, 5, 6):
-            g[i].wait_recv()
-        for i in range(2):
-
-            @pl.when(p < 2 - i)
-            def _():
-                wraps[n][i].start()
-
-        lax.fori_loop(0, PLANE, lambda slot, carry: (convert(n, slot), carry)[1], 0)
+            gathers[n][i].wait_recv()
+        if n > 0:
+            chain_step(n - 1, 2)
+        if n + 1 < NC:
+            third_send(n + 1)
+        convert(n)
         tail_product(n, 4)
         chains[n][0][0].start()
         tail_product(n, 1)
         chains[n][1][0].start()
-        serve()
+        if n > 0:
+            chain_step(n - 1, 3)
+        hub_fill(n)
+        hub_fill_wrap(n)
+        hub_product(n)
         tail_product(n, 3)
         tail_product(n, 2)
-        serve()
+        chain_step(n, 1)
         tail_product(n, 0)
-        for i in range(2):
-
-            @pl.when(p < 2 - i)
-            def _():
-                wraps[n][i].wait_recv()
-                convert(n, 8 + i)
-
-        hub_product(n)
+        if n + 1 < NC:
+            wrap_forward(n + 1)
+        hub_sum(n)
         if n > 0:
-            finish_before = n - 1
-            while pending and pending[0][0] < finish_before:
-                serve()
-        pending.extend((n, s) for s in range(1, 4))
-
-    hub_sum(NC - 1)
-    done = 0
-    while pending:
-        step = pending[0]
-        while done < step[0]:
-            finish(done)
-            done += 1
-        serve()
-    while done < NC:
-        finish(done)
-        done += 1
+            finish(n - 1)
+
+    last = NC - 1
+    chain_step(last, 2)
+    chain_step(last, 3)
+    finish(last)
 
     for n in range(NC):
         for copy in gathers[n]:
@@ -330,12 +375,16 @@
         core_copies[n].wait_send()
         for copy in half_copies[n]:
             copy.wait_send()
-        for i in range(2):
-
-            @pl.when(p < 2 - i)
-            def _():
-                wraps[n][i].wait_send()
-    for copy in tile_copies + meta_copies:
+
+        @pl.when(p < 2)
+        def _():
+            wraps[n].wait_send()
+
+        @pl.when(p == 1)
+        def _():
+            wraps_on[n].wait_send()
+
+    for copy in cross + direct + onward + meta_copies:
         copy.wait_send()
 
 
@@ -368,22 +417,20 @@
         out_specs=vmem,
         scratch_shapes=[
             pltpu.VMEM((NC, 10, ROWS, N), F32),
-            pltpu.VMEM((30, BLOCK, N), BF),
-            pltpu.VMEM((30, BLOCK, N), BF),
+            pltpu.VMEM((24, BLOCK, 2 * N), BF),
             pltpu.VMEM((PLANE, WIN, BLOCK, BLOCK), F32),
+            pltpu.VMEM((NX, WIN, BLOCK, BLOCK), F32),
             pltpu.VMEM((PLANE, WIN, BLOCK, BLOCK), F32),
             pltpu.VMEM((TAILS + 1, BLOCK, BLOCK), F32),
             pltpu.VMEM((PLANE, 8, BLOCK), jnp.int32),
             pltpu.SMEM((PLANE, 8, BLOCK), jnp.int32),
             pltpu.VMEM((5, ROWS, PLANE * BLOCK), BF),
             pltpu.VMEM((5, ROWS, PLANE * BLOCK), BF),
-            pltpu.VMEM((PLANE * BLOCK, N), BF),
-            pltpu.VMEM((PLANE * BLOCK, N), BF),
+            pltpu.VMEM((PLANE * BLOCK, 2 * N), BF),
             pltpu.VMEM((3, 4 * ROWS, ROWS), F32),
             pltpu.VMEM((4 * ROWS, 3 * ROWS), BF),
             pltpu.VMEM((4 * ROWS, 3 * ROWS), BF),
-            pltpu.VMEM((3 * ROWS, N), BF),
-            pltpu.VMEM((3 * ROWS, N), BF),
+            pltpu.VMEM((3 * ROWS, 2 * N), BF),
             pltpu.VMEM((NC, 2, 2, ROWS, N), F32),
             pltpu.VMEM((NC, 2, ROWS, N), F32),
             pltpu.VMEM((NC, ROWS, N), F32),
@@ -395,8 +442,8 @@
             dma((NC + 7,)),
             dma((NC, 7)),
             dma((NC, 7)),
-            dma((7,)),
-            dma((7,)),
+            dma((3, 4)),
+            dma((3, 4)),
             dma((7,)),
             dma((7,)),
             dma((NC,)),

time: 173 us -> 142 us (0.82); the launches traced: 173 us -> 140 us
  Pallas kernels: 167 us -> 134 us
    pallas_call x1, Pallas kernels: 167 us -> 134 us  [per_device(): pl.pallas_call(kernel, out_shape=jax.ShapeDtypeStruct((ROWS, FEAT), F32),...]
where the time goes in v2:
time: 142 us; the launch traced here: 140 us
  Pallas kernels  134 us (94%)
  local copies, waits for them, and re-layouts  4.22 us (3%)
    pallas_call x1, Pallas kernels, per_device(): pl.pallas_call(kernel, out_shape=jax.ShapeDtypeStruct((ROWS, FEAT), F32),...  134 us
    unnamed x2, local copies, waits for them, and re-layouts  3.45 us

profile of v2, /device:TPU:16, one launch (start us, length us, event | category | flops | bytes accessed | tf_op | source)
XLA Modules:
  0.0 140.0 jit_solution(12641693546900127526)
XLA Ops:
  0.0 0.8 fusion.1
  0.8 0.5 broadcast_add_fusion.slot_tile
  1.3 0.1 stack_reshape.6
  1.4 0.1 stack_reshape.7
  1.5 0.6 pad.4.meta
  2.1 1.4 copy.16.mask
  3.5 134.4 %shard_map.73 = f32[384,512]{1,0:T(8,128)} custom-call(f32[384,512]{1,0:T(8,128)} %feat_hbm.1, f32[512,512]{1,0:T(8,128)} %weight_hbm.1, f32[3,1536,384]{2,1,0:T(8,128)} %hub_hbm.1, f32[18,128,128]{2,1,0:T(8,128)} %tail_hbm.1, s32[3,12,3]{2,1,0:T(8,128)} %copy.16.mask, s32[32]{0:T(128)} %broadcast_add_fusion.slot_tile, s32[8,8,128]{2,1,0:T(8,128)} %pad.4.meta), custom_call_target="tpu_custom_call" | custom-call | tf_op jit(solution)/shard_map/pallas_call | solution.py:413
  137.9 2.1 %copy.18 = f32[384,512]{1,0:T(8,128)} copy(f32[384,512]{1,0:T(8,128)} %shard_map.73) | data formatting | bytes 1572864
  (3 shorter events, 0.0 us)

commit v3 on v2

--- a/solution.py
+++ b/solution.py
@@ -17,7 +17,8 @@
 ROWS, FEAT = 384, 512
 NC = 4
 N = FEAT // NC
-SPLIT = 128
+SPLIT = 224
+HOPS = (4, 5)
 BF = jnp.bfloat16
 F32 = jnp.float32
 
@@ -79,7 +80,7 @@
 
     barrier = pltpu.get_barrier_semaphore()
     partners = [at(z, lax.rem(p + i, PLANE)) for i in range(1, PLANE)]
-    partners += [at(z + 1, p), at(z - 1, p), at(z + 4, p), at(z, p, h, 1 - c), at(z, p, 1 - h, c)]
+    partners += [at(z + 1, p), at(z - 1, p), at(z + 3, p), at(z - 3, p), at(z, p, h, 1 - c), at(z, p, 1 - h, c)]
     for dev in partners:
         pl.semaphore_signal(barrier, inc=1, device_id=dev, device_id_type=MESH)
     pl.semaphore_wait(barrier, len(partners))
@@ -201,17 +202,19 @@
     def chain(n, way, s):
         rows = pl.ds(0, size[way])
         src = acc.at[n, order[way][0], pl.ds(part[way].start, size[way])] if s == 0 else zrecv.at[n, way, s - 1, rows]
-        zz = z + 1 if way == 0 else (z - 1 if s < 3 else z + 4)
+        zz = z + 1 if way == 0 else (z - 1 if s < 4 else z - 3)
         return remote(src, zrecv.at[n, way, s, rows], zs.at[n, way, s], zr.at[n, way, s], at(zz, p))
 
-    chains = [[[chain(n, way, s) for s in range(4)] for way in range(2)] for n in range(NC)]
+    chains = [[[chain(n, way, s) for s in range(HOPS[way])] for way in range(2)] for n in range(NC)]
 
     def chain_step(n, s):
         for way in range(2):
-            chains[n][way][s - 1].wait_recv()
-            rows = slice(0, size[way])
-            zrecv[n, way, s - 1, rows] = zrecv[n, way, s - 1, rows] + acc[n, order[way][s], part[way]]
-            chains[n][way][s].start()
+            if s < HOPS[way]:
+                chains[n][way][s - 1].wait_recv()
+                if s < 4:
+                    rows = slice(0, size[way])
+                    zrecv[n, way, s - 1, rows] = zrecv[n, way, s - 1, rows] + acc[n, order[way][s], part[way]]
+                chains[n][way][s].start()
 
     def tail_product(n, d):
         for pp in range(PLANE):
@@ -283,12 +286,12 @@
 
     def finish(n):
         for way in range(2):
-            chains[n][way][3].wait_recv()
+            chains[n][way][-1].wait_recv()
         for copy in half_copies[n]:
             copy.wait_recv()
         for way in range(2):
             rows = part[way]
-            total = (run[n, c, h, rows] + hrecv[n, rows]) + (acc[n, 0, rows] + zrecv[n, way, 3, 0:size[way]])
+            total = (run[n, c, h, rows] + hrecv[n, rows]) + (acc[n, 0, rows] + zrecv[n, way, HOPS[way] - 1, 0:size[way]])
             hi, lo = halves(total)
             cols = slice(n * N, (n + 1) * N)
             value = dot3(hi, lo, wh[cols], wl[cols])
@@ -319,51 +322,82 @@
     scal = pltpu.make_async_copy(mrecv, mscal, load_sem.at[NC + 6])
     scal.start()
     scal.wait()
+    def gathered(n):
+        for i in (2, 3, 5, 6):
+            gathers[n][i].wait_recv()
+
+    def hub_part(n):
+        hub_fill(n)
+        hub_fill_wrap(n)
+        hub_product(n)
+
     build_tile(p)
+    gathered(0)
+    convert(0)
+    hub_part(0)
     for i, dx in enumerate(steps):
         direct[i].wait_recv()
         build_tile(pos(x - dx, y))
+    second_sends(1)
+    first_sends(2)
     cross[3].wait_recv()
     build_tile(yn)
-    second_sends(1)
+    third_send(1)
+    wrap_forward(1)
+    hub_sum(0)
     for i, dx in enumerate(steps):
         onward[i].wait_recv()
         build_tile(pos(x - dx, 1 - y))
 
     for n in range(NC):
-        if n > 0 and n + 1 < NC:
-            second_sends(n + 1)
-        if n + 2 < NC:
-            first_sends(n + 2)
-        for i in (2, 3, 5, 6):
-            gathers[n][i].wait_recv()
         if n > 0:
-            chain_step(n - 1, 2)
-        if n + 1 < NC:
-            third_send(n + 1)
-        convert(n)
+            chain_step(n - 1, 1)
+            if n > 1:
+                chain_step(n - 2, 4)
+            if n + 1 < NC:
+                second_sends(n + 1)
+            gathered(n)
+            convert(n)
         tail_product(n, 4)
         chains[n][0][0].start()
         tail_product(n, 1)
         chains[n][1][0].start()
+        if n == NC - 1:
+            break
         if n > 0:
-            chain_step(n - 1, 3)
-        hub_fill(n)
-        hub_fill_wrap(n)
-        hub_product(n)
+            chain_step(n - 1, 2)
+            third_send(n + 1)
+            if n + 2 < NC:
+                first_sends(n + 2)
+        if n > 0:
+            hub_part(n)
         tail_product(n, 3)
         tail_product(n, 2)
-        chain_step(n, 1)
         tail_product(n, 0)
-        if n + 1 < NC:
+        if n > 0:
             wrap_forward(n + 1)
-        hub_sum(n)
-        if n > 0:
-            finish(n - 1)
+            hub_sum(n)
+            chain_step(n - 1, 3)
+        if n > 1:
+            finish(n - 2)
 
     last = NC - 1
+    tail_product(last, 3)
+    tail_product(last, 2)
+    chain_step(last - 1, 2)
+    hub_fill(last)
+    hub_fill_wrap(last)
+    chain_step(last, 1)
+    hub_product(last)
+    chain_step(last - 1, 3)
     chain_step(last, 2)
+    hub_sum(last)
+    tail_product(last, 0)
+    chain_step(last - 1, 4)
     chain_step(last, 3)
+    finish(last - 2)
+    chain_step(last, 4)
+    finish(last - 1)
     finish(last)
 
     for n in range(NC):
@@ -435,7 +469,7 @@
             pltpu.VMEM((NC, 2, ROWS, N), F32),
             pltpu.VMEM((NC, ROWS, N), F32),
             pltpu.VMEM((NC, 5, ROWS, N), F32),
-            pltpu.VMEM((NC, 2, 4, max(SPLIT, ROWS - SPLIT), N), F32),
+            pltpu.VMEM((NC, 2, 5, max(SPLIT, ROWS - SPLIT), N), F32),
             pltpu.VMEM((FEAT, FEAT), F32),
             pltpu.VMEM((FEAT, FEAT), BF),
             pltpu.VMEM((FEAT, FEAT), BF),
@@ -450,8 +484,8 @@
             dma((NC,)),
             dma((NC, 2)),
             dma((NC, 2)),
-            dma((NC, 2, 4)),
-            dma((NC, 2, 4)),
+            dma((NC, 2, 5)),
+            dma((NC, 2, 5)),
             dma((NC, 2)),
             dma((NC, 2)),
         ],

time: 142 us -> 137 us (0.965)
  the two profiles are of different devices: /device:TPU:16 before, /device:TPU:14 now
where the time goes in v3:
time: 137 us; the launch traced here: 136 us
  Pallas kernels  131 us (96%)
  local copies, waits for them, and re-layouts  4.22 us (3%)
    pallas_call x1, Pallas kernels, per_device(): pl.pallas_call(kernel, out_shape=jax.ShapeDtypeStruct((ROWS, FEAT), F32),...  131 us
    unnamed x2, local copies, waits for them, and re-layouts  3.45 us

profile of v3, /device:TPU:14, one launch (start us, length us, event | category | flops | bytes accessed | tf_op | source)
XLA Modules:
  0.0 136.3 jit_solution(17936705657906547361)
XLA Ops:
  0.0 0.8 fusion.1
  0.8 0.5 broadcast_add_fusion.slot_tile
  1.3 0.1 stack_reshape.6
  1.4 0.1 stack_reshape.7
  1.5 0.6 pad.4.meta
  2.1 1.4 %copy.16.mask = s32[3,12,3]{2,1,0:T(8,128)} copy(s32[3,12,3]{1,2,0:T(4,128)} %param.10) | data formatting | bytes 864 | tf_op args[3]
  3.5 130.7 %shard_map.73 = f32[384,512]{1,0:T(8,128)} custom-call(f32[384,512]{1,0:T(8,128)} %feat_hbm.1, f32[512,512]{1,0:T(8,128)} %weight_hbm.1, f32[3,1536,384]{2,1,0:T(8,128)} %hub_hbm.1, f32[18,128,128]{2,1,0:T(8,128)} %tail_hbm.1, s32[3,12,3]{2,1,0:T(8,128)} %copy.16.mask, s32[32]{0:T(128)} %broadcast_add_fusion.slot_tile, s32[8,8,128]{2,1,0:T(8,128)} %pad.4.meta), custom_call_target="tpu_custom_call" | custom-call | tf_op jit(solution)/shard_map/pallas_call | solution.py:447
  134.3 2.1 %copy.18 = f32[384,512]{1,0:T(8,128)} copy(f32[384,512]{1,0:T(8,128)} %shard_map.73) | data formatting | bytes 1572864
  (3 shorter events, 0.0 us)
